TPU v7x, 128 devices: a whole 4x4x4 slice. The times are simulated.
128 devices in a mesh: req: 16 (over z, y), tp: 8 (over x, core).
Axes of the slice: x: 4, y: 4, z: 4, core: 2. Of those that a mesh axis runs over, the one named last changes fastest.
Arguments:
- new_hidden: bfloat16 [256, 2, 7168], P('req'), may hold values from -6 to 6
- norm_gain: float32 [7168], replicated, may hold values from 0.25 to 1.75
- w_query: bfloat16 [7168, 7168], P(None, 'tp'), may hold values from -8 to 8
- w_key: bfloat16 [7168, 1024], P(None, 'tp'), may hold values from -8 to 8
- w_value: bfloat16 [7168, 1024], P(None, 'tp'), may hold values from -0.0625 to 0.0625
- hidden_store: bfloat16 [16, 409, 7168], P('req'), may hold values from -6 to 6
- key_cache: bfloat16 [16, 4096, 1024], P('req', None, 'tp'), may hold values from -16 to 16
- value_cache: bfloat16 [16, 4096, 1024], P('req', None, 'tp'), may hold values from -6 to 6
- tail_keys: bfloat16 [256, 256, 1024], P('req', None, 'tp'), may hold values from -16 to 16
- tail_values: bfloat16 [256, 256, 1024], P('req', None, 'tp'), may hold values from -6 to 6
- prompt_len: int32 [16], replicated, may hold values from 512 to 4096
- tail_len: int32 [256], P('req'), may hold values from 1 to 256
- recomp_pos: int32 [16, 409], P('req'), may hold values from 0 to 4089, as said below
- cont_prompt: int32 [256, 1], replicated, may hold values from 0 to 15; in each aligned block of 16 rows (0 to 15, 16 to 31, ...) at most 2 rows name the same one
- score_weight: float32 [7168], P('tp'), may hold values from -1.2 to 1.2
Outputs:
- attended: bfloat16 [256, 2, 7168], P('req', None, 'tp')
- scores: float32 [256], P('req')
Inputs may be any that keep to these rules, and one draw needn't show every extreme that they name: recomp_pos[p, j] lies in [10 j, 10 j + 9]. `cont_prompt`: within the rows of one device (aligned blocks of 16 continuations), no prompt is named by more than 2 continuations.
All inputs are finite; a program needn't handle non-finite values.
Results may differ from a plain program's by a relative error of at most 0.0156.
The roundings to bfloat16 on the way count: a program that leaves them out, or rounds other values in their place, can miss the bound.
Values may be sent and summed in bfloat16 or wider, within the bound.
A program may use at most 192 MiB of HBM per device.

v0:
```python
import jax
import jax.numpy as jnp
from jax import lax
from jax.sharding import PartitionSpec as P

HD = 128
MOST = 2


rope_base = 5000000.0


def norm_rows(values, gain):
    widened = values.astype(jnp.float32)
    square = jnp.mean(widened * widened, axis=-1, keepdims=True)
    return (widened * lax.rsqrt(square + 1e-05) * gain).astype(jnp.bfloat16)


def rotate(vector, where_at):
    half = vector.shape[-1] // 2
    freq = rope_base ** (-2.0 * jnp.arange(half, dtype=jnp.float32) / vector.shape[-1])
    angle = where_at.astype(jnp.float32)[..., None] * freq
    first = vector[..., :half]
    second = vector[..., half:]
    return jnp.concatenate(
        [
            first * jnp.cos(angle) - second * jnp.sin(angle),
            second * jnp.cos(angle) + first * jnp.sin(angle),
        ],
        axis=-1,
    )


def set_terms(scores, mask, values, form):
    masked = jnp.where(mask, scores, -1e30)
    top = jnp.max(masked, axis=-1)
    weights = jnp.where(mask, jnp.exp(masked - top[..., None]), 0.0).astype(jnp.bfloat16)
    total = jnp.sum(weights.astype(jnp.float32), axis=-1)
    out = jnp.einsum(form, weights, values, preferred_element_type=jnp.float32)
    return (top, total, out)


def slot_within(prompts):
    count = prompts.shape[-1]
    iota = jnp.arange(count, dtype=jnp.int32)
    same = prompts[..., :, None] == prompts[..., None, :]
    before = iota[None, :] < iota[:, None]
    return jnp.sum((same & before).astype(jnp.int32), axis=-1)


def per_device(
    new_hidden,
    norm_gain,
    w_query,
    w_key,
    w_value,
    hidden_store,
    key_cache,
    value_cache,
    tail_keys,
    tail_values,
    prompt_len,
    tail_len,
    recomp_pos,
    cont_prompt,
    score_weight,
):
    req_rank = lax.axis_index("req")
    cont_dev = new_hidden.shape[0]
    kv_local = w_key.shape[1] // HD
    heads_local = w_query.shape[1] // HD
    group = heads_local // kv_local
    scale = HD ** (-0.5)
    capacity = MOST
    prompts = prompt_len.shape[0]
    prompt_range = jnp.arange(prompts, dtype=jnp.int32)
    ctx = key_cache.shape[1]
    ctx_range = jnp.arange(ctx, dtype=jnp.int32)
    all_prompt = cont_prompt.reshape(-1)
    my_prompt = lax.dynamic_slice_in_dim(all_prompt, req_rank * cont_dev, cont_dev)
    my_slot = slot_within(my_prompt)
    my_index = my_prompt * capacity + my_slot
    local_range = jnp.arange(cont_dev, dtype=jnp.int32)
    my_length = jnp.sum(
        jnp.where(my_prompt[:, None] == prompt_range[None, :], prompt_len[None, :], 0), axis=1
    )
    position = (my_length + tail_len)[:, None] + jnp.arange(2, dtype=jnp.int32)[None, :]
    normed = norm_rows(new_hidden, norm_gain).reshape(cont_dev * 2, -1)
    query = rotate(
        jnp.dot(normed, w_query, preferred_element_type=jnp.float32).reshape(
            cont_dev, 2, heads_local, HD
        ),
        position[..., None],
    ).astype(jnp.bfloat16)
    key_new = rotate(
        jnp.dot(normed, w_key, preferred_element_type=jnp.float32).reshape(
            cont_dev, 2, kv_local, HD
        ),
        position[..., None],
    ).astype(jnp.bfloat16)
    value_new = (
        jnp.dot(normed, w_value, preferred_element_type=jnp.float32)
        .astype(jnp.bfloat16)
        .reshape(cont_dev, 2, kv_local, HD)
    )
    stored = norm_rows(hidden_store[0], norm_gain)
    key_re = (
        rotate(
            jnp.dot(stored, w_key, preferred_element_type=jnp.float32).reshape(-1, kv_local, HD),
            recomp_pos[0][:, None],
        )
        .astype(jnp.bfloat16)
        .reshape(-1, kv_local * HD)
    )
    value_re = jnp.dot(stored, w_value, preferred_element_type=jnp.float32).astype(jnp.bfloat16)
    key_fixed = key_cache[0].at[recomp_pos[0]].set(key_re)
    value_fixed = value_cache[0].at[recomp_pos[0]].set(value_re)
    query_g = query.reshape(cont_dev, 2, kv_local, group, HD)
    tail_count = tail_keys.shape[1]
    tail_s = (
        jnp.einsum(
            "ctkgd,cnkd->ctkgn",
            query_g,
            tail_keys.reshape(cont_dev, tail_count, kv_local, HD),
            preferred_element_type=jnp.float32,
        )
        * scale
    )
    tail_mask = (jnp.arange(tail_count, dtype=jnp.int32)[None, :] < tail_len[:, None])[
        :, None, None, None, :
    ]
    tail = set_terms(
        tail_s,
        tail_mask,
        tail_values.reshape(cont_dev, tail_count, kv_local, HD),
        "ctkgn,cnkd->ctkgd",
    )
    new_s = (
        jnp.einsum("ctkgd,cskd->ctkgs", query_g, key_new, preferred_element_type=jnp.float32)
        * scale
    )
    new_mask = (jnp.arange(2)[None, :] <= jnp.arange(2)[:, None])[None, :, None, None, :]
    fresh = set_terms(new_s, new_mask, value_new, "ctkgs,cskd->ctkgd")
    table = jnp.full((prompts * capacity,), cont_dev, jnp.int32).at[my_index].set(local_range)
    query_pad = jnp.concatenate(
        [query_g, jnp.zeros((1, 2, kv_local, group, HD), query_g.dtype)], axis=0
    )

    def prefix_one(carry, item):
        keys, values, prompt = item
        rows = lax.dynamic_slice_in_dim(table, prompt * capacity, capacity)
        picked = query_pad[rows]
        scores = (
            jnp.einsum(
                "ctkgd,nkd->ctkgn",
                picked,
                keys.reshape(ctx, kv_local, HD),
                preferred_element_type=jnp.float32,
            )
            * scale
        )
        length = jnp.sum(jnp.where(prompt_range == prompt, prompt_len, 0))
        mask = (ctx_range < length)[None, None, None, None, :]
        terms = set_terms(scores, mask, values.reshape(ctx, kv_local, HD), "ctkgn,nkd->ctkgd")
        return (
            (
                carry[0].at[rows].set(terms[0]),
                carry[1].at[rows].set(terms[1]),
                carry[2].at[rows].set(terms[2]),
            ),
            None,
        )

    start_top = jnp.full((cont_dev + 1, 2, kv_local, group), -1e30, jnp.float32)
    start_total = jnp.zeros((cont_dev + 1, 2, kv_local, group), jnp.float32)
    start_out = jnp.zeros((cont_dev + 1, 2, kv_local, group, HD), jnp.float32)
    piece = (
        lax.all_gather(key_fixed[None], "req", axis=0, tiled=True),
        lax.all_gather(value_fixed[None], "req", axis=0, tiled=True),
    )
    count = piece[0].shape[0]
    indices = jnp.arange(count, dtype=jnp.int32)
    folded = lax.scan(
        prefix_one, (start_top, start_total, start_out), (piece[0], piece[1], indices)
    )[0]
    prefix = (folded[0][:cont_dev], folded[1][:cont_dev], folded[2][:cont_dev])
    highest = jnp.maximum(jnp.maximum(prefix[0], tail[0]), fresh[0])
    numer = jnp.zeros((cont_dev, 2, kv_local, group, HD), jnp.float32)
    denom = jnp.zeros((cont_dev, 2, kv_local, group), jnp.float32)
    for part in (prefix, tail, fresh):
        factor = jnp.exp(part[0] - highest)
        numer = numer + factor[..., None] * part[2]
        denom = denom + factor * part[1]
    attended = (
        (numer / denom[..., None]).astype(jnp.bfloat16).reshape(cont_dev, 2, heads_local * HD)
    )
    score_part = jnp.sum(attended[:, 1, :].astype(jnp.float32) * score_weight, axis=-1)
    scores = lax.psum(score_part, "tp")
    return (attended, scores)


def solution(mesh):
    placed = (
        P("req", None, None),
        P(),
        P(None, "tp"),
        P(None, "tp"),
        P(None, "tp"),
        P("req", None, None),
        P("req", None, "tp"),
        P("req", None, "tp"),
        P("req", None, "tp"),
        P("req", None, "tp"),
        P(),
        P("req"),
        P("req", None),
        P(),
        P("tp"),
    )
    return jax.shard_map(
        per_device,
        mesh=mesh,
        in_specs=placed,
        out_specs=(P("req", None, "tp"), P("req")),
        check_vma=False,
    )
```

profile of v0, /device:TPU:1, one launch (start us, length us, event | category | flops | bytes accessed | tf_op | source)
XLA Modules:
  0.0 419.8 jit_solution(5063794833901471259)
XLA Ops:
  9.2 4.2 fusion.14
  13.5 1.8 fusion.26
  16.2 2.3 scatter_custom_fusion.4
  19.5 5.1 %fusion.29 = bf16[409,128]{1,0:T(8,128)(2,1)S(1)} fusion(bf16[7168,128]{1,0:T(8,128)(2,1)} %param.21, bf16[1,409,7168]{2,1,0:T(8,128)(2,1)} %param.22, f32[7168]{0:T(1024)S(1)} %copy-done.8, f32[409]{0:T(512)S(1)} %add_rsqrt_fusion.1), kind=kOutput, calls=%fused_computation.44 | convolution fusion | flops 762297472 | bytes 7833444 | tf_op jit(solution)/shard_map/dot_general | solution.py:115
  24.6 2.3 scatter_fusion.3
  28.0 17.8 %copy.70 = bf16[7168,896]{0,1:T(8,128)(2,1)} copy(bf16[7168,896]{1,0:T(8,128)(2,1)} %param.19) | data formatting | bytes 25690112 | tf_op args[2]
  47.4 6.9 %fusion.50 = f32[16,2,7,128]{3,0,2,1:T(8,128)S(1)} fusion(bf16[7,128,7168,1]{2,1,0,3:T(8,128)(2,1)} %bitcast.250, bf16[16,2,7168,1]{2,1,0,3:T(2,128)(2,1)S(1)} %fusion.107), kind=kOutput, calls=%fused_computation.65 | convolution fusion | flops 411041792 | bytes 13418496 | tf_op jit(solution)/shard_map/dot_general | solution.py:90
  59.3 1.9 convolution_convert_fusion
  61.2 72.8 %all-gather.5.cloned.1.call-done = bf16[65536,128]{1,0:T(8,128)(2,1)} async-done(((bf16[4096,128]{1,0:T(8,128)(2,1)}), bf16[65536,128]{1,0:T(8,128)(2,1)}) %all-gather.5.cloned.1.call-update) | async-done | bytes 16777232 | tf_op jit(solution)/shard_map/all_gather | solution.py:178
  134.1 113.1 %all-gather.7.cloned.1.call-done = bf16[65536,128]{1,0:T(8,128)(2,1)} async-done(((bf16[4096,128]{1,0:T(8,128)(2,1)}), bf16[65536,128]{1,0:T(8,128)(2,1)}) %all-gather.7.cloned.1.call-update) | async-done | bytes 16777232 | tf_op jit(solution)/shard_map/all_gather | solution.py:179
  247.2 150.4 %while.17 = (s32[]{:T(128)}, f32[17,2,1,7]{3,1,0,2:T(2,128)S(1)}, f32[17,2,1,7]{3,1,0,2:T(2,128)S(1)}, f32[17,2,1,7,128]{4,1,3,0,2:T(2,128)S(1)}, s32[16]{0:T(12...) while((s32[]{:T(128)}, f32[17,2,1,7]{3,1,0,2:T(2,128)S(1)}, ...), condition=%wide.region_14.15_spmd.clone.clone, body=%wide.region_7.14_spmd.clone.clone.sunk | while | flops 59986944 | bytes 3603943 | solution.py:183
  260.5 1.8 fusion.117
  269.9 1.8 fusion.117
  279.3 1.8 fusion.117
  288.8 1.8 fusion.117
  298.2 1.8 fusion.117
  307.6 1.8 fusion.117
  317.0 1.8 fusion.117
  326.4 1.8 fusion.117
  335.8 1.8 fusion.117
  354.6 1.8 fusion.117
  373.4 1.8 fusion.117
  392.2 1.8 fusion.117
  399.8 13.1 %psum.7 = f32[16]{0:T(128)} all-reduce(f32[16]{0:T(128)S(1)} %fusion.70), channel_id=1, replica_groups=mesh['req'=16,'tp'=8] {'tp'}, use_global_device_ids=true, to_apply=%region_20.21 | all-reduce | flops 16 | bytes 128 | tf_op jit(solution)/shard_map/psum | solution.py:198
  (270 shorter events, 131.4 us)
Async XLA Ops:
  7.2 6.3 %copy-start = (bf16[7168,128]{1,0:T(8,128)(2,1)S(1)}, bf16[7168,128]{1,0:T(8,128)(2,1)}, u32[]{:S(2)}) copy-start(bf16[7168,128]{1,0:T(8,128)(2,1)} %param.20) | copy-start | bytes 5505028
  7.2 6.3 %copy-start.8 = (f32[7168]{0:T(1024)S(1)}, f32[7168]{0:T(1024)}, u32[]{:S(2)}) copy-start(f32[7168]{0:T(1024)} %param.18) | copy-start | bytes 86020
  7.2 126.9 %all-gather.5.cloned.1.call-start = ((), (), s32[]{:S(2)}) async-start(), calls=%async_computation | async-start | bytes 17825792 | tf_op jit(solution)/shard_map/all_gather | solution.py:178
  7.2 6.2 %copy-start.3 = (bf16[1,409,7168]{2,1,0:T(8,128)(2,1)S(1)}, bf16[1,409,7168]{2,1,0:T(8,128)(2,1)}, u32[]{:S(2)}) copy-start(bf16[1,409,7168]{2,1,0:T(8,128)(2,1)} %param.22) | copy-start | bytes 17590276
  13.4 2.7 copy-start.5
  18.4 1.0 copy-start.4
  19.5 5.1 %copy-start.2 = (bf16[1,4096,128]{2,1,0:T(8,128)(2,1)S(1)}, bf16[1,4096,128]{2,1,0:T(8,128)(2,1)}, u32[]{:S(2)}) copy-start(bf16[1,4096,128]{2,1,0:T(8,128)(2,1)} %param.24) | copy-start | bytes 3145732
  19.5 227.7 %all-gather.7.cloned.1.call-start = ((), (), s32[]{:S(2)}) async-start(), calls=%async_computation.1 | async-start | bytes 17825792 | tf_op jit(solution)/shard_map/all_gather | solution.py:179
  27.0 1.0 copy-start.1
  28.0 17.8 %copy-start.12 = (s32[256,1]{0,1:T(1,128)S(1)}, s32[256,1]{0,1:T(1,128)}, u32[]{:S(2)}) copy-start(s32[256,1]{0,1:T(1,128)} %param.30) | copy-start | bytes 3076
  28.0 17.9 %copy-start.9 = (s32[16]{0:T(128)S(1)}, s32[16]{0:T(128)}, u32[]{:S(2)}) copy-start(s32[16]{0:T(128)} %param.27) | copy-start | bytes 196
  28.0 18.1 %copy-start.11 = (s32[16]{0:T(128)S(1)}, s32[16]{0:T(128)}, u32[]{:S(2)}) copy-start(s32[16]{0:T(128)} %param.28) | copy-start | bytes 196
  28.0 18.1 %copy-start.6 = (bf16[16,2,7168]{2,1,0:T(2,128)(2,1)S(1)}, bf16[16,2,7168]{2,1,0:T(2,128)(2,1)}, u32[]{:S(2)}) copy-start(bf16[16,2,7168]{2,1,0:T(2,128)(2,1)} %param.17) | copy-start | bytes 1376260
  247.2 152.5 %copy-start.10 = (f32[896]{0:T(1024)S(1)}, f32[896]{0:T(1024)}, u32[]{:S(2)}) copy-start(f32[896]{0:T(1024)} %param.31) | copy-start | bytes 10756
  399.6 13.3 %copy-start.7 = (bf16[16,2,896]{2,1,0:T(2,128)(2,1)}, bf16[16,2,896]{2,1,0:T(2,128)(2,1)S(1)}, u32[]{:S(2)}) copy-start(bf16[16,2,896]{2,1,0:T(2,128)(2,1)S(1)} %reshape.537) | copy-start | bytes 172036
Sparse Core Ops, SparseCore 0:
  19.6 114.4 all-gather.4
  136.2 110.9 all-gather.6
where the time goes:
time: 423 us; the launch traced here: 420 us
  waiting for transfers between devices  186 us (44%)
  matrix products  73.3 us (17%)
  local copies, waits for them, and re-layouts  70.7 us (17%)
  other arithmetic  50.7 us (12%)
  between operations  14.4 us (3%)
  blocking collectives  13.1 us (3%)
  loops' own time  11.5 us (3%)
    all_gather x1, waiting for transfers between devices, per_device(): lax.all_gather(value_fixed[None], 'req', axis=0, tiled=True)  113 us
    all_gather x1, waiting for transfers between devices, per_device(): lax.all_gather(key_fixed[None], 'req', axis=0, tiled=True)  72.8 us
    dot_general x16, matrix products, prefix_one(): jnp.einsum('ctkgd,nkd->ctkgn', picked, keys.reshape(ctx, kv_local, HD), p...  28.2 us
    dot_general x18, matrix products, set_terms(): out = jnp.einsum(form, weights, values, preferred_element_type=jnp.float32)  26.9 us
    reduce_sum x16, other arithmetic, prefix_one(): length = jnp.sum(jnp.where(prompt_range == prompt, prompt_len, 0))  21.5 us
    unnamed x28, local copies, waits for them, and re-layouts  19.9 us
    psum x1, blocking collectives, per_device(): scores = lax.psum(score_part, 'tp')  13.1 us
    another operation x1, loops' own time, per_device(): lax.scan(prefix_one, (start_top, start_total, start_out), (piece[0], piec...  11.5 us
  transfers between devices with their start and end apart: 2, of which 2 were waited for; matrix products, arithmetic and copies ran while one was open for 10% of the time, Pallas kernels for 0%

commit v1 on v0

v1 whole, which is shorter than its diff:
```python
import functools
import math

import jax
import jax.numpy as jnp
import numpy as np
from jax import lax
from jax.experimental import pallas as pl
from jax.experimental.pallas import tpu as pltpu
from jax.sharding import PartitionSpec as P

MESH = pl.DeviceIdType.MESH
HD = 128
NEG = -1e30
THETA = 5000000.0
LOG2E = math.log2(math.e)
F32 = jnp.float32
BF16 = jnp.bfloat16
I32 = jnp.int32


def iota(shape, dim):
    return lax.broadcasted_iota(I32, shape, dim)


def dot(a, b):
    return jnp.dot(a, b, preferred_element_type=F32)


def dot_t(a, b):
    return lax.dot_general(a, b, (((1,), (1,)), ((), ())), preferred_element_type=F32)


def onehot(mask):
    return jnp.where(mask, 1.0, 0.0).astype(BF16)


def kernel(
    dims,
    nh_hbm,
    gain_ref,
    wq_hbm,
    wk_hbm,
    wv_hbm,
    hs_hbm,
    kc_hbm,
    vc_hbm,
    tk_hbm,
    tv_hbm,
    plen_ref,
    tlen_ref,
    rpos_ref,
    cont_ref,
    sw_ref,
    freq_ref,
    out_ref,
    score_ref,
    nh,
    wq,
    w,
    hs,
    sn,
    kk,
    vv,
    tk,
    tv,
    pos_row,
    posb,
    ropec,
    ropes,
    bias,
    qacc,
    kvacc,
    qs,
    qt,
    xs,
    rq,
    s_buf,
    rs,
    rr,
    st,
    to,
    scs,
    scr,
    in_sem,
    wq_sem,
    qsend,
    qrecv,
    rsend,
    rrecv,
    ssend,
    srecv,
):
    n_req, n_tp, inner, D, CTX, TAIL, RECOMP, CD, G = dims
    T = 2
    ROWS = CD * T
    RP = -(-RECOMP // 32) * 32
    KT = kk.shape[0]
    outer = n_req // inner
    me = lax.axis_index("req")
    mt = lax.axis_index("tp")
    scale = HD ** (-0.5) * LOG2E
    CH = wq.shape[1]
    n_ch = wq.shape[0]

    load_nh = pltpu.make_async_copy(nh_hbm, nh, in_sem.at[0])
    load_nh.start()
    loads_q = [
        pltpu.make_async_copy(wq_hbm.at[pl.ds(i * CH, CH)], wq.at[i], wq_sem.at[i])
        for i in range(n_ch)
    ]
    for copy in loads_q:
        copy.start()
    load_wk = pltpu.make_async_copy(wk_hbm, w.at[:, pl.ds(0, HD)], in_sem.at[1])
    load_wv = pltpu.make_async_copy(wv_hbm, w.at[:, pl.ds(HD, HD)], in_sem.at[2])
    load_hs = pltpu.make_async_copy(hs_hbm.at[0], hs, in_sem.at[3])
    load_kc = pltpu.make_async_copy(kc_hbm.at[0], kk.at[pl.ds(0, CTX)], in_sem.at[4])
    load_vc = pltpu.make_async_copy(
        vc_hbm.at[0], vv.at[pl.ds(0, CTX), pl.ds(0, HD)], in_sem.at[5]
    )
    load_tk = pltpu.make_async_copy(tk_hbm, tk, in_sem.at[6])
    load_tv = pltpu.make_async_copy(tv_hbm, tv, in_sem.at[7])
    for copy in (load_hs, load_wk, load_wv, load_kc, load_vc, load_tk, load_tv):
        copy.start()

    barrier = pltpu.get_barrier_semaphore()
    for k in range(1, n_req):
        pl.semaphore_signal(
            barrier, inc=1, device_id={"req": lax.rem(me + k, n_req)}, device_id_type=MESH
        )
    for k in range(1, n_tp):
        pl.semaphore_signal(
            barrier, inc=1, device_id={"tp": lax.rem(mt + k, n_tp)}, device_id_type=MESH
        )

    crow = cont_ref[...]
    pcol = jnp.sum(
        jnp.where(iota((CD, crow.shape[1]), 1) == me * CD + iota((CD, crow.shape[1]), 0), crow, 0),
        axis=1,
        keepdims=True,
    )
    eye = iota((CD, HD), 0) == iota((CD, HD), 1)
    prow = jnp.sum(jnp.where(eye, pcol, 0), axis=0, keepdims=True)
    earlier = (prow == pcol) & (iota((CD, HD), 1) < iota((CD, HD), 0))
    slot = jnp.sum(jnp.where(earlier, 1, 0), axis=1, keepdims=True)
    base = pcol * 32 + slot * 16
    KR = CD * 16
    trow = jnp.sum(
        jnp.where(iota((CD, KR), 0) == iota((CD, KR), 1) // 16, base, 0), axis=0, keepdims=True
    ) + lax.rem(iota((1, KR), 1), 16)
    brow = jnp.sum(jnp.where(eye, base, 0), axis=0, keepdims=True)
    own = iota((KR, HD), 1) == iota((KR, HD), 0) // 16
    tcol = jnp.sum(jnp.where(own, brow, 0), axis=1, keepdims=True) + lax.rem(
        iota((KR, 1), 0), 16
    )

    n_p = plen_ref.shape[1]
    plen = plen_ref[...]
    tlen = tlen_ref[...]
    clen = jnp.sum(
        jnp.where(iota((CD, n_p), 1) == pcol, plen, 0), axis=1, keepdims=True
    ) + jnp.sum(jnp.where(iota((CD, CD), 0) == iota((CD, CD), 1), tlen, 0), axis=1, keepdims=True)
    lrow = jnp.sum(jnp.where(eye, clen, 0), axis=0, keepdims=True)
    pos_new = jnp.sum(
        jnp.where(iota((ROWS, HD), 1) == iota((ROWS, HD), 0) // T, lrow, 0), axis=1, keepdims=True
    ) + lax.rem(iota((ROWS, 1), 0), T)
    freq = freq_ref[...]
    sign = jnp.where(iota((1, HD), 1) < HD // 2, -1.0, 1.0)
    angle = pos_new.astype(F32) * freq
    cos_new = jnp.cos(angle)
    sin_new = jnp.sin(angle) * sign

    def norm_block(load, store):
        total = None
        for j in range(0, D, 512):
            x = load(j).astype(F32)
            x = x * x
            for i in range(0, 512, HD):
                total = x[:, i : i + HD] if total is None else total + x[:, i : i + HD]
        factor = lax.rsqrt(jnp.sum(total, axis=1, keepdims=True) * (1.0 / D) + 1e-05)
        for j in range(0, D, 512):
            x = load(j).astype(F32)
            store(j, x * factor * gain_ref[:, j : j + 512])

    load_nh.wait()
    for r in range(0, ROWS, 16):

        def load_new(j, r=r):
            return nh[r : r + 16, j : j + 512]

        def store_new(j, x, r=r):
            sn[RP + r : RP + r + 16, j : j + 512] = x.astype(BF16)

        norm_block(load_new, store_new)

    NB = posb.shape[0]
    pos_row[...] = jnp.full(pos_row.shape, -1, I32)
    pos_row[:, 0:RECOMP] = rpos_ref[...]
    for j in range(0, NB, HD):
        chunk = pos_row[:, j : j + HD].astype(F32)
        posb[j : j + HD, :] = jnp.transpose(jnp.broadcast_to(chunk, (HD, HD)))

    def tables(i, carry):
        at = pl.ds(pl.multiple_of(i * 16, 16), 16)
        turned = posb[at, :] * freq
        ropec[at, :] = jnp.cos(turned)
        ropes[at, :] = jnp.sin(turned) * sign
        return carry

    lax.fori_loop(0, RP // 16, tables, 0)
    my_len = jnp.sum(jnp.where(iota((1, n_p), 1) == me, plen, 0), axis=1, keepdims=True).astype(F32)
    for b in range(0, CTX, HD):
        first = b // 10 // 8 * 8
        rows = min(24, NB - first)
        here = (b + iota((1, HD), 1)).astype(F32)
        same = jnp.where(posb[first : first + rows, :] == here, 1.0, 0.0)
        replaced = jnp.max(same, axis=0, keepdims=True)
        bias[:, b : b + HD] = jnp.where((replaced > 0.0) | (here >= my_len), NEG, 0.0)
    for b in range(0, KT - CTX, HD):
        if b < NB:
            at = pos_row[:, b : b + HD].astype(F32)
            bias[:, CTX + b : CTX + b + HD] = jnp.where((at < 0.0) | (at >= my_len), NEG, 0.0)
        else:
            bias[:, CTX + b : CTX + b + HD] = jnp.full((1, HD), NEG, F32)
    vv[:, HD:] = jnp.ones((KT, HD), BF16)
    kk[CTX:, :] = jnp.zeros((KT - CTX, HD), BF16)
    vv[CTX:, 0:HD] = jnp.zeros((KT - CTX, HD), BF16)

    qacc[...] = jnp.zeros_like(qacc)

    def query_chunk(i, carry):
        pltpu.make_async_copy(wq_hbm.at[pl.ds(0, CH)], wq.at[i], wq_sem.at[i]).wait()
        x = sn[RP : RP + ROWS, pl.ds(pl.multiple_of(i * CH, CH), CH)]
        qacc[...] += dot(x, wq[i])
        return carry

    lax.fori_loop(0, n_ch, query_chunk, 0)
    for g in range(G):
        x = qacc[:, g * HD : (g + 1) * HD]
        x = x * cos_new + pltpu.roll(x, HD // 2, 1) * sin_new
        qs[g * ROWS : (g + 1) * ROWS, :] = x.astype(BF16)
    krow = iota((KR, G * ROWS), 0)
    picks = (lax.rem(krow, 16) // T) * ROWS + (krow // 16) * T + lax.rem(krow, T)
    qt[...] = dot(onehot(iota((KR, G * ROWS), 1) == picks), qs[...]).astype(BF16)
    n_x = n_req * 32
    sent = dot(onehot(iota((n_x, KR), 0) == trow), qt[...]).astype(BF16)
    for p in range(n_req):
        xs[p] = sent[p * 32 : (p + 1) * 32]

    pl.semaphore_wait(barrier, n_req + n_tp - 2)

    def peer(k):
        z = lax.rem(me // inner + k // inner, outer)
        y = lax.rem(lax.rem(me, inner) + lax.rem(k, inner), inner)
        return z * inner + y

    def query_copy(slot_at, to_dev):
        return pltpu.make_async_remote_copy(
            src_ref=xs.at[slot_at],
            dst_ref=rq.at[me],
            send_sem=qsend.at[slot_at],
            recv_sem=qrecv.at[me],
            device_id={"req": to_dev},
            device_id_type=MESH,
        )

    def query_arrival(src):
        return pltpu.make_async_remote_copy(
            src_ref=xs.at[src],
            dst_ref=rq.at[src],
            send_sem=qsend.at[src],
            recv_sem=qrecv.at[src],
            device_id={"req": src},
            device_id_type=MESH,
        )

    for k in range(1, n_req):
        to_dev = lax.rem(me + k, n_req)
        query_copy(to_dev, to_dev).start()
    rq[me] = xs[me]

    load_hs.wait()

    def stored_block(i, carry):
        at = pl.ds(pl.multiple_of(i * 16, 16), 16)

        def load_old(j):
            return hs[at, j : j + 512]

        def store_old(j, x):
            sn[at, j : j + 512] = x.astype(BF16)

        norm_block(load_old, store_old)
        return carry

    lax.fori_loop(0, RECOMP // 16, stored_block, 0)
    if RECOMP < RP:
        last = RECOMP // 16 * 16
        sn[last:RP, :] = jnp.zeros((RP - last, D), BF16)
        if last < RECOMP:

            def load_last(j):
                return hs[last:RECOMP, j : j + 512]

            def store_last(j, x):
                sn[last:RECOMP, j : j + 512] = x.astype(BF16)

            norm_block(load_last, store_last)
    load_wk.wait()
    load_wv.wait()
    kvacc[...] = jnp.zeros_like(kvacc)

    def kv_chunk(i, carry):
        at = pl.ds(pl.multiple_of(i * CH, CH), CH)
        kvacc[...] += dot(sn[:, at], w[at, :])
        return carry

    lax.fori_loop(0, D // CH, kv_chunk, 0)
    x = kvacc[0:RP, 0:HD]
    x = x * ropec[0:RP, :] + pltpu.roll(x, HD // 2, 1) * ropes[0:RP, :]
    load_kc.wait()
    load_vc.wait()
    kk[CTX : CTX + RP, :] = x.astype(BF16)
    vv[CTX : CTX + RP, 0:HD] = kvacc[0:RP, HD:].astype(BF16)
    x = kvacc[RP : RP + ROWS, 0:HD]
    key_new = (x * cos_new + pltpu.roll(x, HD // 2, 1) * sin_new).astype(BF16)
    value_new = kvacc[RP : RP + ROWS, HD:].astype(BF16)

    BC = 512
    NS = inner
    NR = NS * 32

    def prefix_block(i, carry):
        peers = [peer(n_req - 1 - i * NS - j) for j in range(NS)]
        for j in range(NS):

            @pl.when((i < n_req // NS - 1) | (j < NS - 1))
            def _(j=j):
                query_arrival(peers[j]).wait_recv()

        q = jnp.concatenate([rq[p] for p in peers], axis=0)
        top = None
        for j in range(0, KT, BC):
            s = dot_t(q, kk[j : j + BC, :]) + bias[:, j : j + BC]
            s_buf[:, j : j + BC] = s
            for b in range(0, BC, HD):
                part = s[:, b : b + HD]
                top = part if top is None else jnp.maximum(top, part)
        high = jnp.max(top, axis=1, keepdims=True) * scale
        acc = jnp.zeros((NR, 2 * HD), F32)
        for j in range(0, KT, BC):
            weights = jnp.exp2(s_buf[:, j : j + BC] * scale - high).astype(BF16)
            acc = acc + dot(weights, vv[j : j + BC, :])
        total = acc[:, HD:]
        out = acc[:, 0:HD] / total
        lse = jnp.transpose(high + jnp.log2(total))
        row = iota((32, HD), 0)
        for j in range(NS):
            stat = lse[0:32, :]
            if j:
                stat = pltpu.roll(stat, HD - 32 * j, 1)
            first = stat.astype(BF16).astype(F32)
            second = (stat - first).astype(BF16).astype(F32)
            third = stat - first - second
            block = jnp.where(
                row == 14,
                first,
                jnp.where(row == 15, second, jnp.where(row == 30, third, out[32 * j : 32 * j + 32])),
            )
            rs[peers[j]] = block.astype(BF16)
        for j in range(NS):

            @pl.when((i < n_req // NS - 1) | (j < NS - 1))
            def _(j=j):
                pltpu.make_async_remote_copy(
                    src_ref=rs.at[peers[j]],
                    dst_ref=rr.at[me],
                    send_sem=rsend.at[peers[j]],
                    recv_sem=rrecv.at[me],
                    device_id={"req": peers[j]},
                    device_id_type=MESH,
                ).start()

        return carry

    lax.fori_loop(0, n_req // NS, prefix_block, 0)
    rr[me] = rs[me]

    load_tk.wait()
    load_tv.wait()

    def tail_scores(c, carry):
        at = pl.ds(pl.multiple_of(c * 16, 16), 16)
        st[at, :] = dot_t(qt[at, :], tk[c])
        return carry

    lax.fori_loop(0, CD, tail_scores, 0)
    tlcol = jnp.sum(
        jnp.where(iota((KR, CD), 1) == iota((KR, CD), 0) // 16, tlen, 0), axis=1, keepdims=True
    )
    mask = iota((KR, TAIL), 1) < tlcol
    s = jnp.where(mask, st[...], NEG)
    m_t = jnp.max(s, axis=1, keepdims=True) * scale
    weights = jnp.where(mask, jnp.exp2(s * scale - m_t), 0.0).astype(BF16).astype(F32)
    l_t = jnp.sum(weights, axis=1, keepdims=True)
    st[...] = weights

    def tail_out(c, carry):
        at = pl.ds(pl.multiple_of(c * 16, 16), 16)
        to[at, :] = dot(st[at, :].astype(BF16), tv[c])
        return carry

    lax.fori_loop(0, CD, tail_out, 0)

    q32 = qt[...].astype(F32)
    hrow = iota((KR, ROWS), 0)
    odd = lax.rem(iota((KR, 1), 0), T) == 1
    pick0 = onehot(iota((KR, ROWS), 1) == (hrow // 16) * T)
    pick1 = onehot(iota((KR, ROWS), 1) == (hrow // 16) * T + 1)
    s0 = jnp.sum(q32 * dot(pick0, key_new), axis=1, keepdims=True) * scale
    s1 = jnp.where(odd, jnp.sum(q32 * dot(pick1, key_new), axis=1, keepdims=True) * scale, NEG)
    m_f = jnp.maximum(s0, s1)
    w0 = jnp.exp2(s0 - m_f).astype(BF16).astype(F32)
    w1 = jnp.where(odd, jnp.exp2(s1 - m_f), 0.0).astype(BF16).astype(F32)
    l_f = w0 + w1
    o_f = w0 * dot(pick0, value_new) + w1 * dot(pick1, value_new)

    for k in range(1, n_req):
        src = lax.rem(me + k, n_req)
        pltpu.make_async_remote_copy(
            src_ref=rs.at[src],
            dst_ref=rr.at[src],
            send_sem=rsend.at[src],
            recv_sem=rrecv.at[src],
            device_id={"req": src},
            device_id_type=MESH,
        ).wait_recv()
    parts = jnp.concatenate([rr[p] for p in range(n_req)], axis=0)
    lane = iota((KR, n_x), 1)
    o_p = dot(onehot(lane == tcol), parts)
    inside = lax.rem(lane, 32)
    stat_at = ((inside == 14) | (inside == 15) | (inside == 30)) & (lane // 32 == tcol // 32)
    stats = dot(onehot(stat_at), parts)
    lse_p = jnp.sum(
        jnp.where(iota((KR, HD), 1) == lax.rem(tcol, 32), stats, 0.0), axis=1, keepdims=True
    )

    top = jnp.maximum(jnp.maximum(lse_p, m_t), m_f)
    f_p = jnp.exp2(lse_p - top)
    f_t = jnp.exp2(m_t - top)
    f_f = jnp.exp2(m_f - top)
    numer = f_p * o_p + f_t * to[...] + f_f * o_f
    denom = f_p + f_t * l_t + f_f * l_f
    attended = (numer / denom).astype(BF16)
    brow2 = iota((G * ROWS, KR), 0)
    back = (lax.rem(brow2, ROWS) // T) * 16 + (brow2 // ROWS) * T + lax.rem(brow2, T)
    final = dot(onehot(iota((G * ROWS, KR), 1) == back), attended)
    partial = jnp.zeros((ROWS, HD), F32)
    for g in range(G):
        x = final[g * ROWS : (g + 1) * ROWS]
        out_ref[:, g * HD : (g + 1) * HD] = x.astype(BF16)
        partial = partial + x * sw_ref[:, g * HD : (g + 1) * HD]
    column = jnp.sum(partial, axis=1, keepdims=True)
    line = jnp.sum(
        jnp.where(iota((ROWS, HD), 0) == iota((ROWS, HD), 1) * T + 1, column, 0.0),
        axis=0,
        keepdims=True,
    )
    line = jnp.broadcast_to(line, (8, HD))
    scs[...] = line
    scr[mt] = line

    def score_copy(slot_at, k, dev):
        return pltpu.make_async_remote_copy(
            src_ref=scs,
            dst_ref=scr.at[slot_at],
            send_sem=ssend.at[k],
            recv_sem=srecv.at[slot_at],
            device_id={"tp": dev},
            device_id_type=MESH,
        )

    for k in range(1, n_tp):
        score_copy(mt, k, lax.rem(mt + k, n_tp)).start()
    for k in range(1, n_tp):
        src = lax.rem(mt + k, n_tp)
        score_copy(src, k, src).wait_recv()
    total = scr[0]
    for k in range(1, n_tp):
        total = total + scr[k]
    score_ref[...] = total

    for k in range(1, n_tp):
        dev = lax.rem(mt + k, n_tp)
        score_copy(dev, k, dev).wait_send()
    for k in range(1, n_req):
        dev = lax.rem(me + k, n_req)
        query_copy(dev, dev).wait_send()
        pltpu.make_async_remote_copy(
            src_ref=rs.at[dev],
            dst_ref=rr.at[me],
            send_sem=rsend.at[dev],
            recv_sem=rrecv.at[me],
            device_id={"req": dev},
            device_id_type=MESH,
        ).wait_send()


def per_device(
    inner,
    n_req,
    n_tp,
    new_hidden,
    norm_gain,
    w_query,
    w_key,
    w_value,
    hidden_store,
    key_cache,
    value_cache,
    tail_keys,
    tail_values,
    prompt_len,
    tail_len,
    recomp_pos,
    cont_prompt,
    score_weight,
):
    CD, T, D = new_hidden.shape
    QW = w_query.shape[1]
    G = QW // HD
    CTX = key_cache.shape[1]
    TAIL = tail_keys.shape[1]
    RECOMP = hidden_store.shape[1]
    ROWS = CD * T
    RP = -(-RECOMP // 32) * 32
    NB = -(-RECOMP // HD) * HD
    KT = CTX + 512
    CH = 512
    KR = CD * 16
    NR = inner * 32
    half = HD // 2
    freq = THETA ** (-2.0 * np.arange(half, dtype=np.float64) / HD)
    freq = np.concatenate([freq, freq]).astype(np.float32)[None, :]
    dims = (n_req, n_tp, inner, D, CTX, TAIL, RECOMP, CD, G)
    hbm = pl.BlockSpec(memory_space=pl.ANY)
    vmem = pl.BlockSpec(memory_space=pltpu.VMEM)
    dma = pltpu.SemaphoreType.DMA
    attended, scores = pl.pallas_call(
        functools.partial(kernel, dims),
        out_shape=(
            jax.ShapeDtypeStruct((ROWS, QW), BF16),
            jax.ShapeDtypeStruct((8, HD), F32),
        ),
        in_specs=[hbm, vmem] + [hbm] * 8 + [vmem] * 6,
        out_specs=(vmem, vmem),
        scratch_shapes=[
            pltpu.VMEM((ROWS, D), BF16),
            pltpu.VMEM((D // CH, CH, QW), BF16),
            pltpu.VMEM((D, 2 * HD), BF16),
            pltpu.VMEM((RECOMP, D), BF16),
            pltpu.VMEM((RP + ROWS, D), BF16),
            pltpu.VMEM((KT, HD), BF16),
            pltpu.VMEM((KT, 2 * HD), BF16),
            pltpu.VMEM((CD, TAIL, HD), BF16),
            pltpu.VMEM((CD, TAIL, HD), BF16),
            pltpu.VMEM((1, NB), I32),
            pltpu.VMEM((NB, HD), F32),
            pltpu.VMEM((RP, HD), F32),
            pltpu.VMEM((RP, HD), F32),
            pltpu.VMEM((1, KT), F32),
            pltpu.VMEM((ROWS, QW), F32),
            pltpu.VMEM((RP + ROWS, 2 * HD), F32),
            pltpu.VMEM((G * ROWS, HD), BF16),
            pltpu.VMEM((KR, HD), BF16),
            pltpu.VMEM((n_req, 32, HD), BF16),
            pltpu.VMEM((n_req, 32, HD), BF16),
            pltpu.VMEM((NR, KT), F32),
            pltpu.VMEM((n_req, 32, HD), BF16),
            pltpu.VMEM((n_req, 32, HD), BF16),
            pltpu.VMEM((KR, TAIL), F32),
            pltpu.VMEM((KR, HD), F32),
            pltpu.VMEM((8, HD), F32),
            pltpu.VMEM((n_tp, 8, HD), F32),
            dma((8,)),
            dma((D // CH,)),
            dma((n_req,)),
            dma((n_req,)),
            dma((n_req,)),
            dma((n_req,)),
            dma((n_tp,)),
            dma((n_tp,)),
        ],
        compiler_params=pltpu.CompilerParams(
            collective_id=0, has_side_effects=True, vmem_limit_bytes=56 * 1024 * 1024
        ),
        name="decode",
    )(
        new_hidden.reshape(ROWS, D),
        norm_gain.reshape(1, D),
        w_query,
        w_key,
        w_value,
        hidden_store,
        key_cache,
        value_cache,
        tail_keys,
        tail_values,
        prompt_len.reshape(1, -1),
        tail_len.reshape(1, -1),
        recomp_pos,
        cont_prompt.reshape(1, -1),
        score_weight.reshape(1, -1),
        jnp.asarray(freq),
    )
    return attended.reshape(CD, T, QW), scores[0, :CD]


def solution(mesh):
    placed = (
        P("req", None, None),
        P(),
        P(None, "tp"),
        P(None, "tp"),
        P(None, "tp"),
        P("req", None, None),
        P("req", None, "tp"),
        P("req", None, "tp"),
        P("req", None, "tp"),
        P("req", None, "tp"),
        P(),
        P("req"),
        P("req", None),
        P(),
        P("tp"),
    )
    n_req = mesh.shape["req"]
    inner = 4 if n_req % 4 == 0 else 1
    return jax.shard_map(
        functools.partial(per_device, inner, n_req, mesh.shape["tp"]),
        mesh=mesh,
        in_specs=placed,
        out_specs=(P("req", None, "tp"), P("req")),
        check_vma=False,
    )
```

time: 423 us -> 48.7 us (0.12)
  waiting for transfers between devices: 186 us -> 0 us
  matrix products: 73.3 us -> 0 us
  local copies, waits for them, and re-layouts: 70.7 us -> 5.87 us
  other arithmetic: 50.7 us -> 0 us
  Pallas kernels: 0 us -> 41.8 us
  between operations: 14.4 us -> 0.64 us
  blocking collectives: 13.1 us -> 0 us
  loops' own time: 11.5 us -> 0 us
    all_gather x2 -> x0, waiting for transfers between devices: 186 us -> none  [the longest x1 113 us: per_device(): lax.all_gather(value_fixed[None], 'req', axis=0, tiled=True)]
    dot_general x41 -> x0, matrix products: 73.3 us -> none  [the longest x16 28.2 us: prefix_one(): jnp.einsum('ctkgd,nkd->ctkgn', picked, keys.reshape(ctx, kv_local, HD), p...]
    pallas_call x0 -> x1, Pallas kernels: none -> 41.8 us  [per_device(): pl.pallas_call(functools.partial(kernel, dims), out_shape=(jax.ShapeDtype...]
    scatter x50 -> x0, local copies, waits for them, and re-layouts: 32 us -> none  [the longest x16 9.85 us: prefix_one(): carry[2].at[rows].set(terms[2])]
    reduce_sum x38 -> x0, other arithmetic: 31.3 us -> none  [the longest x16 21.5 us: prefix_one(): length = jnp.sum(jnp.where(prompt_range == prompt, prompt_len, 0))]
    unnamed x28 -> x0, local copies, waits for them, and re-layouts: 19.9 us -> none
    psum x1 -> x0, blocking collectives: 13.1 us -> none  [per_device(): scores = lax.psum(score_part, 'tp')]
    another operation x1 -> x0, loops' own time: 11.5 us -> none  [per_device(): lax.scan(prefix_one, (start_top, start_total, start_out), (piece[0], piec...]
  transfers between devices with their start and end apart: 2 -> 0, of which waited for: 2 -> 0; matrix products, arithmetic and copies ran while one was open for 10% -> 0% of each run, Pallas kernels for 0% -> 0%
where the time goes in v1:
time: 48.7 us; the launch traced here: 48.3 us
  Pallas kernels  41.8 us (86%)
  local copies, waits for them, and re-layouts  5.87 us (12%)
  between operations  0.64 us (1%)
    pallas_call x1, Pallas kernels, per_device(): pl.pallas_call(functools.partial(kernel, dims), out_shape=(jax.ShapeDtype...  41.8 us
    reshape x1, local copies, waits for them, and re-layouts, per_device(): new_hidden.reshape(ROWS, D)  1.95 us
    reshape x1, local copies, waits for them, and re-layouts, per_device(): return (attended.reshape(CD, T, QW), scores[0, :CD])  1.47 us
    reshape x1, local copies, waits for them, and re-layouts, per_device(): score_weight.reshape(1, -1)  1.27 us
    squeeze x1, local copies, waits for them, and re-layouts, per_device(): return (attended.reshape(CD, T, QW), scores[0, :CD])  1.18 us

profile of v1, /device:TPU:1, one launch (start us, length us, event | category | flops | bytes accessed | tf_op | source)
XLA Modules:
  0.0 48.3 jit_solution(15758786361480782399)
XLA Ops:
  0.6 1.3 %reshape.30.sw_ref = f32[1,896]{1,0:T(1,128)} reshape(f32[896]{0:T(1024)} %param.30) | data formatting | bytes 7168 | tf_op jit(solution)/shard_map/reshape | solution.py:613
  1.9 2.0 %reshape.25.nh_hbm = bf16[32,7168]{1,0:T(8,128)(2,1)} reshape(bf16[16,2,7168]{2,1,0:T(2,128)(2,1)} %param.16) | data formatting | bytes 917504 | tf_op jit(solution)/shard_map/reshape | solution.py:599
  3.9 41.8 %decode.1 = (bf16[32,896]{1,0:T(8,128)(2,1)}, f32[8,128]{1,0:T(8,128)}) custom-call(bf16[32,7168]{1,0:T(8,128)(2,1)} %reshape.25.nh_hbm, f32[1,7168]{1,0:T(1,128)} %bitcast.6, bf16[7168,896]{1,0:T(8,128)(2,1)} %wq_hbm.1, bf16[7168,128]{1,0:T(8,128)(2,1)} %wk_hbm.1, bf16[7168,128]{1,0:T(8,128)(2,1)} %wv_hbm.1, bf16[1,409,7168]{2,1,0:T(8,128)(2,1)} %hs_hbm.1, ...), custom_call_target="tpu_custom_call" | custom-call | tf_op jit(solution)/shard_map/decode/pallas_call | solution.py:549
  45.7 1.5 %reshape.31 = bf16[16,2,896]{2,1,0:T(2,128)(2,1)} reshape(bf16[32,896]{1,0:T(8,128)(2,1)} %get-tuple-element.4) | data formatting | bytes 114688 | tf_op jit(solution)/shard_map/reshape | solution.py:616
  47.1 1.2 %slice_bitcast_fusion = f32[16]{0:T(128)} fusion(f32[8,128]{1,0:T(8,128)} %get-tuple-element.5), kind=kLoop, calls=%fused_computation | loop fusion | bytes 128 | tf_op jit(solution)/shard_map/squeeze | solution.py:616

commit v2 on v1

--- a/solution.py
+++ b/solution.py
@@ -38,7 +38,7 @@
 def kernel(
     dims,
     nh_hbm,
-    gain_ref,
+    gain_hbm,
     wq_hbm,
     wk_hbm,
     wv_hbm,
@@ -47,15 +47,22 @@
     vc_hbm,
     tk_hbm,
     tv_hbm,
+    plen_hbm,
+    tlen_hbm,
+    rpos_hbm,
+    cont_hbm,
+    sw_hbm,
+    freq_hbm,
+    out_ref,
+    score_ref,
+    nh,
+    gain_ref,
     plen_ref,
     tlen_ref,
     rpos_ref,
     cont_ref,
     sw_ref,
     freq_ref,
-    out_ref,
-    score_ref,
-    nh,
     wq,
     w,
     hs,
@@ -83,6 +90,7 @@
     scs,
     scr,
     in_sem,
+    nh_sem,
     wq_sem,
     qsend,
     qrecv,
@@ -103,13 +111,31 @@
     CH = wq.shape[1]
     n_ch = wq.shape[0]
 
-    load_nh = pltpu.make_async_copy(nh_hbm, nh, in_sem.at[0])
-    load_nh.start()
+    loads_nh = [
+        pltpu.make_async_copy(nh_hbm.at[c], nh.at[pl.ds(c * T, T)], nh_sem.at[c]) for c in range(CD)
+    ]
+    for copy in loads_nh:
+        copy.start()
+    small = (
+        (gain_hbm, gain_ref),
+        (plen_hbm, plen_ref),
+        (tlen_hbm, tlen_ref),
+        (rpos_hbm, rpos_ref),
+        (cont_hbm, cont_ref),
+        (sw_hbm, sw_ref),
+        (freq_hbm, freq_ref),
+    )
+    loads_small = [
+        pltpu.make_async_copy(src, dst, in_sem.at[8 + i]) for i, (src, dst) in enumerate(small)
+    ]
+    for copy in loads_small:
+        copy.start()
     loads_q = [
         pltpu.make_async_copy(wq_hbm.at[pl.ds(i * CH, CH)], wq.at[i], wq_sem.at[i])
         for i in range(n_ch)
     ]
-    for copy in loads_q:
+    DEPTH = min(6, n_ch)
+    for copy in loads_q[:DEPTH]:
         copy.start()
     load_wk = pltpu.make_async_copy(wk_hbm, w.at[:, pl.ds(0, HD)], in_sem.at[1])
     load_wv = pltpu.make_async_copy(wv_hbm, w.at[:, pl.ds(HD, HD)], in_sem.at[2])
@@ -120,8 +146,7 @@
     )
     load_tk = pltpu.make_async_copy(tk_hbm, tk, in_sem.at[6])
     load_tv = pltpu.make_async_copy(tv_hbm, tv, in_sem.at[7])
-    for copy in (load_hs, load_wk, load_wv, load_kc, load_vc, load_tk, load_tv):
-        copy.start()
+    after = loads_q[DEPTH:] + [load_hs, load_wk, load_wv, load_kc, load_vc, load_tk, load_tv]
 
     barrier = pltpu.get_barrier_semaphore()
     for k in range(1, n_req):
@@ -133,6 +158,13 @@
             barrier, inc=1, device_id={"tp": lax.rem(mt + k, n_tp)}, device_id_type=MESH
         )
 
+    vv[:, HD:] = jnp.ones((KT, HD), BF16)
+    kk[CTX:, :] = jnp.zeros((KT - CTX, HD), BF16)
+    vv[CTX:, 0:HD] = jnp.zeros((KT - CTX, HD), BF16)
+
+    for copy in loads_small:
+        copy.wait()
+
     crow = cont_ref[...]
     pcol = jnp.sum(
         jnp.where(iota((CD, crow.shape[1]), 1) == me * CD + iota((CD, crow.shape[1]), 0), crow, 0),
@@ -145,9 +177,13 @@
     slot = jnp.sum(jnp.where(earlier, 1, 0), axis=1, keepdims=True)
     base = pcol * 32 + slot * 16
     KR = CD * 16
+    QR = G * ROWS
+    qcol = iota((1, QR), 1)
     trow = jnp.sum(
-        jnp.where(iota((CD, KR), 0) == iota((CD, KR), 1) // 16, base, 0), axis=0, keepdims=True
-    ) + lax.rem(iota((1, KR), 1), 16)
+        jnp.where(iota((CD, QR), 0) == lax.rem(iota((CD, QR), 1), ROWS) // T, base, 0),
+        axis=0,
+        keepdims=True,
+    ) + (qcol // ROWS * T + lax.rem(qcol, T))
     brow = jnp.sum(jnp.where(eye, base, 0), axis=0, keepdims=True)
     own = iota((KR, HD), 1) == iota((KR, HD), 0) // 16
     tcol = jnp.sum(jnp.where(own, brow, 0), axis=1, keepdims=True) + lax.rem(
@@ -182,16 +218,70 @@
             x = load(j).astype(F32)
             store(j, x * factor * gain_ref[:, j : j + 512])
 
-    load_nh.wait()
-    for r in range(0, ROWS, 16):
+    for copy in loads_nh:
+        copy.wait()
+    for r in range(0, ROWS, ROWS):
 
         def load_new(j, r=r):
-            return nh[r : r + 16, j : j + 512]
+            return nh[r : r + ROWS, j : j + 512]
 
         def store_new(j, x, r=r):
-            sn[RP + r : RP + r + 16, j : j + 512] = x.astype(BF16)
+            sn[RP + r : RP + r + ROWS, j : j + 512] = x.astype(BF16)
 
         norm_block(load_new, store_new)
+
+    for i in range(n_ch):
+        loads_q[i].wait()
+        for copy in after[i : i + 1] if i < n_ch - 1 else after[i:]:
+            copy.start()
+        part = dot(sn[RP : RP + ROWS, i * CH : (i + 1) * CH], wq[i])
+        if i == 0:
+            qacc[...] = part
+        else:
+            qacc[...] += part
+    for g in range(G):
+        x = qacc[:, g * HD : (g + 1) * HD]
+        x = x * cos_new + pltpu.roll(x, HD // 2, 1) * sin_new
+        qs[g * ROWS : (g + 1) * ROWS, :] = x.astype(BF16)
+    n_x = n_req * 32
+    sent = dot(onehot(iota((n_x, QR), 0) == trow), qs[...]).astype(BF16)
+    for p in range(n_req):
+        xs[p] = sent[p * 32 : (p + 1) * 32]
+
+    pl.semaphore_wait(barrier, n_req + n_tp - 2)
+
+    def peer(k):
+        z = lax.rem(me // inner + k // inner, outer)
+        y = lax.rem(lax.rem(me, inner) + lax.rem(k, inner), inner)
+        return z * inner + y
+
+    def query_copy(slot_at, to_dev):
+        return pltpu.make_async_remote_copy(
+            src_ref=xs.at[slot_at],
+            dst_ref=rq.at[me],
+            send_sem=qsend.at[slot_at],
+            recv_sem=qrecv.at[me],
+            device_id={"req": to_dev},
+            device_id_type=MESH,
+        )
+
+    def query_arrival(src):
+        return pltpu.make_async_remote_copy(
+            src_ref=xs.at[src],
+            dst_ref=rq.at[src],
+            send_sem=qsend.at[src],
+            recv_sem=qrecv.at[src],
+            device_id={"req": src},
+            device_id_type=MESH,
+        )
+
+    for k in range(1, n_req):
+        to_dev = lax.rem(me + k, n_req)
+        query_copy(to_dev, to_dev).start()
+    rq[me] = xs[me]
+    krow = iota((KR, G * ROWS), 0)
+    picks = (lax.rem(krow, 16) // T) * ROWS + (krow // 16) * T + lax.rem(krow, T)
+    qt[...] = dot(onehot(iota((KR, G * ROWS), 1) == picks), qs[...]).astype(BF16)
 
     NB = posb.shape[0]
     pos_row[...] = jnp.full(pos_row.shape, -1, I32)
@@ -222,67 +312,13 @@
             bias[:, CTX + b : CTX + b + HD] = jnp.where((at < 0.0) | (at >= my_len), NEG, 0.0)
         else:
             bias[:, CTX + b : CTX + b + HD] = jnp.full((1, HD), NEG, F32)
-    vv[:, HD:] = jnp.ones((KT, HD), BF16)
-    kk[CTX:, :] = jnp.zeros((KT - CTX, HD), BF16)
-    vv[CTX:, 0:HD] = jnp.zeros((KT - CTX, HD), BF16)
-
-    qacc[...] = jnp.zeros_like(qacc)
-
-    def query_chunk(i, carry):
-        pltpu.make_async_copy(wq_hbm.at[pl.ds(0, CH)], wq.at[i], wq_sem.at[i]).wait()
-        x = sn[RP : RP + ROWS, pl.ds(pl.multiple_of(i * CH, CH), CH)]
-        qacc[...] += dot(x, wq[i])
-        return carry
-
-    lax.fori_loop(0, n_ch, query_chunk, 0)
-    for g in range(G):
-        x = qacc[:, g * HD : (g + 1) * HD]
-        x = x * cos_new + pltpu.roll(x, HD // 2, 1) * sin_new
-        qs[g * ROWS : (g + 1) * ROWS, :] = x.astype(BF16)
-    krow = iota((KR, G * ROWS), 0)
-    picks = (lax.rem(krow, 16) // T) * ROWS + (krow // 16) * T + lax.rem(krow, T)
-    qt[...] = dot(onehot(iota((KR, G * ROWS), 1) == picks), qs[...]).astype(BF16)
-    n_x = n_req * 32
-    sent = dot(onehot(iota((n_x, KR), 0) == trow), qt[...]).astype(BF16)
-    for p in range(n_req):
-        xs[p] = sent[p * 32 : (p + 1) * 32]
-
-    pl.semaphore_wait(barrier, n_req + n_tp - 2)
-
-    def peer(k):
-        z = lax.rem(me // inner + k // inner, outer)
-        y = lax.rem(lax.rem(me, inner) + lax.rem(k, inner), inner)
-        return z * inner + y
-
-    def query_copy(slot_at, to_dev):
-        return pltpu.make_async_remote_copy(
-            src_ref=xs.at[slot_at],
-            dst_ref=rq.at[me],
-            send_sem=qsend.at[slot_at],
-            recv_sem=qrecv.at[me],
-            device_id={"req": to_dev},
-            device_id_type=MESH,
-        )
-
-    def query_arrival(src):
-        return pltpu.make_async_remote_copy(
-            src_ref=xs.at[src],
-            dst_ref=rq.at[src],
-            send_sem=qsend.at[src],
-            recv_sem=qrecv.at[src],
-            device_id={"req": src},
-            device_id_type=MESH,
-        )
-
-    for k in range(1, n_req):
-        to_dev = lax.rem(me + k, n_req)
-        query_copy(to_dev, to_dev).start()
-    rq[me] = xs[me]
 
     load_hs.wait()
 
+    NB_ROWS = 80 if RECOMP >= 80 else 16
+
     def stored_block(i, carry):
-        at = pl.ds(pl.multiple_of(i * 16, 16), 16)
+        at = pl.ds(pl.multiple_of(i * NB_ROWS, 16), NB_ROWS)
 
         def load_old(j):
             return hs[at, j : j + 512]
@@ -293,9 +329,9 @@
         norm_block(load_old, store_old)
         return carry
 
-    lax.fori_loop(0, RECOMP // 16, stored_block, 0)
+    lax.fori_loop(0, RECOMP // NB_ROWS, stored_block, 0)
     if RECOMP < RP:
-        last = RECOMP // 16 * 16
+        last = RECOMP // NB_ROWS * NB_ROWS
         sn[last:RP, :] = jnp.zeros((RP - last, D), BF16)
         if last < RECOMP:
 
@@ -308,14 +344,15 @@
             norm_block(load_last, store_last)
     load_wk.wait()
     load_wv.wait()
-    kvacc[...] = jnp.zeros_like(kvacc)
+    KC = D // 4
+    kvacc[...] = dot(sn[:, 0:KC], w[0:KC, :])
 
     def kv_chunk(i, carry):
-        at = pl.ds(pl.multiple_of(i * CH, CH), CH)
+        at = pl.ds(pl.multiple_of(i * KC, HD), KC)
         kvacc[...] += dot(sn[:, at], w[at, :])
         return carry
 
-    lax.fori_loop(0, D // CH, kv_chunk, 0)
+    lax.fori_loop(1, 4, kv_chunk, 0)
     x = kvacc[0:RP, 0:HD]
     x = x * ropec[0:RP, :] + pltpu.roll(x, HD // 2, 1) * ropes[0:RP, :]
     load_kc.wait()
@@ -327,7 +364,7 @@
     value_new = kvacc[RP : RP + ROWS, HD:].astype(BF16)
 
     BC = 512
-    NS = inner
+    NS = 2 * inner
     NR = NS * 32
 
     def prefix_block(i, carry):
@@ -353,12 +390,13 @@
             acc = acc + dot(weights, vv[j : j + BC, :])
         total = acc[:, HD:]
         out = acc[:, 0:HD] / total
-        lse = jnp.transpose(high + jnp.log2(total))
+        lse = high + jnp.log2(total)
+        lses = [jnp.transpose(lse[r : r + HD]) for r in range(0, NR, HD)]
         row = iota((32, HD), 0)
         for j in range(NS):
-            stat = lse[0:32, :]
-            if j:
-                stat = pltpu.roll(stat, HD - 32 * j, 1)
+            stat = lses[32 * j // HD][0:32, :]
+            if 32 * j % HD:
+                stat = pltpu.roll(stat, HD - 32 * j % HD, 1)
             first = stat.astype(BF16).astype(F32)
             second = (stat - first).astype(BF16).astype(F32)
             third = stat - first - second
@@ -394,7 +432,7 @@
         st[at, :] = dot_t(qt[at, :], tk[c])
         return carry
 
-    lax.fori_loop(0, CD, tail_scores, 0)
+    lax.fori_loop(0, CD, tail_scores, 0, unroll=True)
     tlcol = jnp.sum(
         jnp.where(iota((KR, CD), 1) == iota((KR, CD), 0) // 16, tlen, 0), axis=1, keepdims=True
     )
@@ -410,7 +448,7 @@
         to[at, :] = dot(st[at, :].astype(BF16), tv[c])
         return carry
 
-    lax.fori_loop(0, CD, tail_out, 0)
+    lax.fori_loop(0, CD, tail_out, 0, unroll=True)
 
     q32 = qt[...].astype(F32)
     hrow = iota((KR, ROWS), 0)
@@ -459,7 +497,7 @@
     for g in range(G):
         x = final[g * ROWS : (g + 1) * ROWS]
         out_ref[:, g * HD : (g + 1) * HD] = x.astype(BF16)
-        partial = partial + x * sw_ref[:, g * HD : (g + 1) * HD]
+        partial = partial + x * sw_ref[pl.ds(g * HD, HD)].reshape(1, HD)
     column = jnp.sum(partial, axis=1, keepdims=True)
     line = jnp.sum(
         jnp.where(iota((ROWS, HD), 0) == iota((ROWS, HD), 1) * T + 1, column, 0.0),
@@ -538,7 +576,7 @@
     KT = CTX + 512
     CH = 512
     KR = CD * 16
-    NR = inner * 32
+    NR = 2 * inner * 32
     half = HD // 2
     freq = THETA ** (-2.0 * np.arange(half, dtype=np.float64) / HD)
     freq = np.concatenate([freq, freq]).astype(np.float32)[None, :]
@@ -552,10 +590,17 @@
             jax.ShapeDtypeStruct((ROWS, QW), BF16),
             jax.ShapeDtypeStruct((8, HD), F32),
         ),
-        in_specs=[hbm, vmem] + [hbm] * 8 + [vmem] * 6,
+        in_specs=[hbm] * 16,
         out_specs=(vmem, vmem),
         scratch_shapes=[
             pltpu.VMEM((ROWS, D), BF16),
+            pltpu.VMEM((1, D), F32),
+            pltpu.VMEM((1, prompt_len.shape[0]), I32),
+            pltpu.VMEM((1, CD), I32),
+            pltpu.VMEM((1, RECOMP), I32),
+            pltpu.VMEM((1, cont_prompt.shape[0]), I32),
+            pltpu.VMEM((QW,), F32),
+            pltpu.VMEM((1, HD), F32),
             pltpu.VMEM((D // CH, CH, QW), BF16),
             pltpu.VMEM((D, 2 * HD), BF16),
             pltpu.VMEM((RECOMP, D), BF16),
@@ -582,7 +627,8 @@
             pltpu.VMEM((KR, HD), F32),
             pltpu.VMEM((8, HD), F32),
             pltpu.VMEM((n_tp, 8, HD), F32),
-            dma((8,)),
+            dma((15,)),
+            dma((CD,)),
             dma((D // CH,)),
             dma((n_req,)),
             dma((n_req,)),
@@ -592,11 +638,11 @@
             dma((n_tp,)),
         ],
         compiler_params=pltpu.CompilerParams(
-            collective_id=0, has_side_effects=True, vmem_limit_bytes=56 * 1024 * 1024
+            collective_id=0, has_side_effects=True, vmem_limit_bytes=67_043_328
         ),
         name="decode",
     )(
-        new_hidden.reshape(ROWS, D),
+        new_hidden,
         norm_gain.reshape(1, D),
         w_query,
         w_key,
@@ -610,7 +656,7 @@
         tail_len.reshape(1, -1),
         recomp_pos,
         cont_prompt.reshape(1, -1),
-        score_weight.reshape(1, -1),
+        score_weight,
         jnp.asarray(freq),
     )
     return attended.reshape(CD, T, QW), scores[0, :CD]

time: 48.7 us -> 41.3 us (0.85)
  Pallas kernels: 41.8 us -> 37.8 us
  local copies, waits for them, and re-layouts: 5.87 us -> 2.66 us
    pallas_call x1, Pallas kernels: 41.8 us -> 37.8 us  [per_device(): pl.pallas_call(functools.partial(kernel, dims), out_shape=(jax.ShapeDtype...]
    reshape x2 -> x0, local copies, waits for them, and re-layouts: 3.22 us -> none  [the longest x1 1.95 us: per_device(): new_hidden.reshape(ROWS, D)]
where the time goes in v2:
time: 41.3 us; the launch traced here: 41.1 us
  Pallas kernels  37.8 us (92%)
  local copies, waits for them, and re-layouts  2.66 us (6%)
  between operations  0.64 us (2%)
    pallas_call x1, Pallas kernels, per_device(): pl.pallas_call(functools.partial(kernel, dims), out_shape=(jax.ShapeDtype...  37.8 us
    reshape x1, local copies, waits for them, and re-layouts, per_device(): return (attended.reshape(CD, T, QW), scores[0, :CD])  1.47 us
    squeeze x1, local copies, waits for them, and re-layouts, per_device(): return (attended.reshape(CD, T, QW), scores[0, :CD])  1.19 us

profile of v2, /device:TPU:1, one launch (start us, length us, event | category | flops | bytes accessed | tf_op | source)
XLA Modules:
  0.0 41.1 jit_solution(9316868733684535699)
XLA Ops:
  0.6 37.8 %decode.1 = (bf16[32,896]{1,0:T(8,128)(2,1)}, f32[8,128]{1,0:T(8,128)}) custom-call(bf16[16,2,7168]{2,1,0:T(2,128)(2,1)} %nh_hbm.1, f32[1,7168]{1,0:T(1,128)} %bitcast.6, bf16[7168,896]{1,0:T(8,128)(2,1)} %wq_hbm.1, bf16[7168,128]{1,0:T(8,128)(2,1)} %wk_hbm.1, bf16[7168,128]{1,0:T(8,128)(2,1)} %wv_hbm.1, bf16[1,409,7168]{2,1,0:T(8,128)(2,1)} %hs_hbm.1, ...), custom_call_target="tpu_custom_call" | custom-call | tf_op jit(solution)/shard_map/decode/pallas_call | solution.py:587
  38.5 1.5 %reshape.23 = bf16[16,2,896]{2,1,0:T(2,128)(2,1)} reshape(bf16[32,896]{1,0:T(8,128)(2,1)} %get-tuple-element.4) | data formatting | bytes 114688 | tf_op jit(solution)/shard_map/reshape | solution.py:662
  39.9 1.2 %slice_bitcast_fusion = f32[16]{0:T(128)} fusion(f32[8,128]{1,0:T(8,128)} %get-tuple-element.5), kind=kLoop, calls=%fused_computation | loop fusion | bytes 128 | tf_op jit(solution)/shard_map/squeeze | solution.py:662

commit v3 on v2

--- a/solution.py
+++ b/solution.py
@@ -89,6 +89,11 @@
     to,
     scs,
     scr,
+    pick_o,
+    pick_s,
+    pick_b,
+    outv,
+    out_sem,
     in_sem,
     nh_sem,
     wq_sem,
@@ -363,31 +368,35 @@
     key_new = (x * cos_new + pltpu.roll(x, HD // 2, 1) * sin_new).astype(BF16)
     value_new = kvacc[RP : RP + ROWS, HD:].astype(BF16)
 
-    BC = 512
+    BC = 256
+    RR = HD
     NS = 2 * inner
     NR = NS * 32
 
-    def prefix_block(i, carry):
+    def prefix_block(i):
         peers = [peer(n_req - 1 - i * NS - j) for j in range(NS)]
         for j in range(NS):
 
-            @pl.when((i < n_req // NS - 1) | (j < NS - 1))
-            def _(j=j):
+            if i < n_req // NS - 1 or j < NS - 1:
                 query_arrival(peers[j]).wait_recv()
 
         q = jnp.concatenate([rq[p] for p in peers], axis=0)
         top = None
         for j in range(0, KT, BC):
             s = dot_t(q, kk[j : j + BC, :]) + bias[:, j : j + BC]
-            s_buf[:, j : j + BC] = s
+            s_buf[i, :, j : j + BC] = s
             for b in range(0, BC, HD):
                 part = s[:, b : b + HD]
                 top = part if top is None else jnp.maximum(top, part)
         high = jnp.max(top, axis=1, keepdims=True) * scale
-        acc = jnp.zeros((NR, 2 * HD), F32)
-        for j in range(0, KT, BC):
-            weights = jnp.exp2(s_buf[:, j : j + BC] * scale - high).astype(BF16)
-            acc = acc + dot(weights, vv[j : j + BC, :])
+        accs = []
+        for r in range(0, NR, RR):
+            acc = jnp.zeros((RR, 2 * HD), F32)
+            for j in range(0, KT, BC):
+                x = s_buf[i, r : r + RR, j : j + BC] * scale - high[r : r + RR]
+                acc = acc + dot(jnp.exp2(x).astype(BF16), vv[j : j + BC, :])
+            accs.append(acc)
+        acc = jnp.concatenate(accs, axis=0)
         total = acc[:, HD:]
         out = acc[:, 0:HD] / total
         lse = high + jnp.log2(total)
@@ -408,8 +417,7 @@
             rs[peers[j]] = block.astype(BF16)
         for j in range(NS):
 
-            @pl.when((i < n_req // NS - 1) | (j < NS - 1))
-            def _(j=j):
+            if i < n_req // NS - 1 or j < NS - 1:
                 pltpu.make_async_remote_copy(
                     src_ref=rs.at[peers[j]],
                     dst_ref=rr.at[me],
@@ -419,9 +427,8 @@
                     device_id_type=MESH,
                 ).start()
 
-        return carry
-
-    lax.fori_loop(0, n_req // NS, prefix_block, 0)
+    for i in range(n_req // NS):
+        prefix_block(i)
     rr[me] = rs[me]
 
     load_tk.wait()
@@ -463,6 +470,14 @@
     l_f = w0 + w1
     o_f = w0 * dot(pick0, value_new) + w1 * dot(pick1, value_new)
 
+    lane = iota((KR, n_x), 1)
+    inside = lax.rem(lane, 32)
+    stat_at = ((inside == 14) | (inside == 15) | (inside == 30)) & (lane // 32 == tcol // 32)
+    pick_o[...] = onehot(lane == tcol)
+    pick_s[...] = onehot(stat_at)
+    brow2 = iota((G * ROWS, KR), 0)
+    back = (lax.rem(brow2, ROWS) // T) * 16 + (brow2 // ROWS) * T + lax.rem(brow2, T)
+    pick_b[...] = onehot(iota((G * ROWS, KR), 1) == back)
     for k in range(1, n_req):
         src = lax.rem(me + k, n_req)
         pltpu.make_async_remote_copy(
@@ -474,11 +489,8 @@
             device_id_type=MESH,
         ).wait_recv()
     parts = jnp.concatenate([rr[p] for p in range(n_req)], axis=0)
-    lane = iota((KR, n_x), 1)
-    o_p = dot(onehot(lane == tcol), parts)
-    inside = lax.rem(lane, 32)
-    stat_at = ((inside == 14) | (inside == 15) | (inside == 30)) & (lane // 32 == tcol // 32)
-    stats = dot(onehot(stat_at), parts)
+    o_p = dot(pick_o[...], parts)
+    stats = dot(pick_s[...], parts)
     lse_p = jnp.sum(
         jnp.where(iota((KR, HD), 1) == lax.rem(tcol, 32), stats, 0.0), axis=1, keepdims=True
     )
@@ -490,14 +502,14 @@
     numer = f_p * o_p + f_t * to[...] + f_f * o_f
     denom = f_p + f_t * l_t + f_f * l_f
     attended = (numer / denom).astype(BF16)
-    brow2 = iota((G * ROWS, KR), 0)
-    back = (lax.rem(brow2, ROWS) // T) * 16 + (brow2 // ROWS) * T + lax.rem(brow2, T)
-    final = dot(onehot(iota((G * ROWS, KR), 1) == back), attended)
+    final = dot(pick_b[...], attended)
     partial = jnp.zeros((ROWS, HD), F32)
     for g in range(G):
         x = final[g * ROWS : (g + 1) * ROWS]
-        out_ref[:, g * HD : (g + 1) * HD] = x.astype(BF16)
+        outv[:, g * HD : (g + 1) * HD] = x.astype(BF16)
         partial = partial + x * sw_ref[pl.ds(g * HD, HD)].reshape(1, HD)
+    store_out = pltpu.make_async_copy(outv, out_ref, out_sem)
+    store_out.start()
     column = jnp.sum(partial, axis=1, keepdims=True)
     line = jnp.sum(
         jnp.where(iota((ROWS, HD), 0) == iota((ROWS, HD), 1) * T + 1, column, 0.0),
@@ -527,6 +539,8 @@
     for k in range(1, n_tp):
         total = total + scr[k]
     score_ref[...] = total
+
+    store_out.wait()
 
     for k in range(1, n_tp):
         dev = lax.rem(mt + k, n_tp)
@@ -542,6 +556,13 @@
             device_id={"req": dev},
             device_id_type=MESH,
         ).wait_send()
+
+
+def finish(rows_ref, line_ref, out_ref, score_ref):
+    CD, T = out_ref.shape[:2]
+    for c in range(CD):
+        out_ref[c] = rows_ref[c * T : (c + 1) * T, :]
+    score_ref[...] = line_ref[0, 0:CD]
 
 
 def per_device(
@@ -591,7 +612,7 @@
             jax.ShapeDtypeStruct((8, HD), F32),
         ),
         in_specs=[hbm] * 16,
-        out_specs=(vmem, vmem),
+        out_specs=(hbm, vmem),
         scratch_shapes=[
             pltpu.VMEM((ROWS, D), BF16),
             pltpu.VMEM((1, D), F32),
@@ -620,13 +641,18 @@
             pltpu.VMEM((KR, HD), BF16),
             pltpu.VMEM((n_req, 32, HD), BF16),
             pltpu.VMEM((n_req, 32, HD), BF16),
-            pltpu.VMEM((NR, KT), F32),
+            pltpu.VMEM((n_req * 32 // NR, NR, KT), F32),
             pltpu.VMEM((n_req, 32, HD), BF16),
             pltpu.VMEM((n_req, 32, HD), BF16),
             pltpu.VMEM((KR, TAIL), F32),
             pltpu.VMEM((KR, HD), F32),
             pltpu.VMEM((8, HD), F32),
             pltpu.VMEM((n_tp, 8, HD), F32),
+            pltpu.VMEM((KR, n_req * 32), BF16),
+            pltpu.VMEM((KR, n_req * 32), BF16),
+            pltpu.VMEM((G * ROWS, KR), BF16),
+            pltpu.VMEM((ROWS, QW), BF16),
+            dma,
             dma((15,)),
             dma((CD,)),
             dma((D // CH,)),
@@ -659,7 +685,17 @@
         score_weight,
         jnp.asarray(freq),
     )
-    return attended.reshape(CD, T, QW), scores[0, :CD]
+    return pl.pallas_call(
+        finish,
+        out_shape=(
+            jax.ShapeDtypeStruct((CD, T, QW), BF16),
+            jax.ShapeDtypeStruct((CD,), F32),
+        ),
+        in_specs=[vmem, vmem],
+        out_specs=(vmem, vmem),
+        compiler_params=pltpu.CompilerParams(vmem_limit_bytes=67_043_328),
+        name="finish",
+    )(attended, scores)
 
 
 def solution(mesh):

time: 41.3 us -> 37.6 us (0.910)
  local copies, waits for them, and re-layouts: 2.66 us -> 0 us
  Pallas kernels: 37.8 us -> 36.7 us
    pallas_call x1, Pallas kernels: 37.8 us -> 35.3 us  [per_device(): pl.pallas_call(functools.partial(kernel, dims), out_shape=(jax.ShapeDtype...]
    pallas_call x0 -> x1, Pallas kernels: none -> 1.49 us  [per_device(): pl.pallas_call(finish, out_shape=(jax.ShapeDtypeStruct((CD, T, QW), BF16)...]
    reshape x1 -> x0, local copies, waits for them, and re-layouts: 1.47 us -> none  [per_device(): return (attended.reshape(CD, T, QW), scores[0, :CD])]
    squeeze x1 -> x0, local copies, waits for them, and re-layouts: 1.19 us -> none  [per_device(): return (attended.reshape(CD, T, QW), scores[0, :CD])]
where the time goes in v3:
time: 37.6 us; the launch traced here: 37.4 us
  Pallas kernels  36.7 us (98%)
  between operations  0.64 us (2%)
    pallas_call x1, Pallas kernels, per_device(): pl.pallas_call(functools.partial(kernel, dims), out_shape=(jax.ShapeDtype...  35.3 us
    pallas_call x1, Pallas kernels, per_device(): pl.pallas_call(finish, out_shape=(jax.ShapeDtypeStruct((CD, T, QW), BF16)...  1.49 us

profile of v3, /device:TPU:1, one launch (start us, length us, event | category | flops | bytes accessed | tf_op | source)
XLA Modules:
  0.0 37.4 jit_solution(6160404397329868944)
XLA Ops:
  0.6 35.3 %decode.1 = (bf16[32,896]{1,0:T(8,128)(2,1)}, f32[8,128]{1,0:T(8,128)}) custom-call(bf16[16,2,7168]{2,1,0:T(2,128)(2,1)} %nh_hbm.1, f32[1,7168]{1,0:T(1,128)} %bitcast.4, bf16[7168,896]{1,0:T(8,128)(2,1)} %wq_hbm.1, bf16[7168,128]{1,0:T(8,128)(2,1)} %wk_hbm.1, bf16[7168,128]{1,0:T(8,128)(2,1)} %wv_hbm.1, bf16[1,409,7168]{2,1,0:T(8,128)(2,1)} %hs_hbm.1, ...), custom_call_target="tpu_custom_call" | custom-call | tf_op jit(solution)/shard_map/decode/pallas_call | solution.py:608
  35.9 1.5 %finish.1 = (bf16[16,2,896]{2,1,0:T(2,128)(2,1)}, f32[16]{0:T(128)}) custom-call(bf16[32,896]{1,0:T(8,128)(2,1)} %get-tuple-element.4.rows_ref, f32[8,128]{1,0:T(8,128)} %get-tuple-element.5.line_ref), custom_call_target="tpu_custom_call" | custom-call | tf_op jit(solution)/shard_map/finish/pallas_call | solution.py:688

commit v4 on v3

--- a/solution.py
+++ b/solution.py
@@ -170,6 +170,39 @@
     for copy in loads_small:
         copy.wait()
 
+    def norm_block(load, store):
+        total = None
+        for j in range(0, D, 512):
+            x = load(j).astype(F32)
+            x = x * x
+            for i in range(0, 512, HD):
+                total = x[:, i : i + HD] if total is None else total + x[:, i : i + HD]
+        factor = lax.rsqrt(jnp.sum(total, axis=1, keepdims=True) * (1.0 / D) + 1e-05)
+        for j in range(0, D, 512):
+            x = load(j).astype(F32)
+            store(j, x * factor * gain_ref[:, j : j + 512])
+
+    for copy in loads_nh:
+        copy.wait()
+    for r in range(0, ROWS, ROWS):
+
+        def load_new(j, r=r):
+            return nh[r : r + ROWS, j : j + 512]
+
+        def store_new(j, x, r=r):
+            sn[RP + r : RP + r + ROWS, j : j + 512] = x.astype(BF16)
+
+        norm_block(load_new, store_new)
+
+    for i in range(n_ch):
+        loads_q[i].wait()
+        for copy in after[i : i + 1] if i < n_ch - 1 else after[i:]:
+            copy.start()
+        part = dot(sn[RP : RP + ROWS, i * CH : (i + 1) * CH], wq[i])
+        if i == 0:
+            qacc[...] = part
+        else:
+            qacc[...] += part
     crow = cont_ref[...]
     pcol = jnp.sum(
         jnp.where(iota((CD, crow.shape[1]), 1) == me * CD + iota((CD, crow.shape[1]), 0), crow, 0),
@@ -211,39 +244,6 @@
     cos_new = jnp.cos(angle)
     sin_new = jnp.sin(angle) * sign
 
-    def norm_block(load, store):
-        total = None
-        for j in range(0, D, 512):
-            x = load(j).astype(F32)
-            x = x * x
-            for i in range(0, 512, HD):
-                total = x[:, i : i + HD] if total is None else total + x[:, i : i + HD]
-        factor = lax.rsqrt(jnp.sum(total, axis=1, keepdims=True) * (1.0 / D) + 1e-05)
-        for j in range(0, D, 512):
-            x = load(j).astype(F32)
-            store(j, x * factor * gain_ref[:, j : j + 512])
-
-    for copy in loads_nh:
-        copy.wait()
-    for r in range(0, ROWS, ROWS):
-
-        def load_new(j, r=r):
-            return nh[r : r + ROWS, j : j + 512]
-
-        def store_new(j, x, r=r):
-            sn[RP + r : RP + r + ROWS, j : j + 512] = x.astype(BF16)
-
-        norm_block(load_new, store_new)
-
-    for i in range(n_ch):
-        loads_q[i].wait()
-        for copy in after[i : i + 1] if i < n_ch - 1 else after[i:]:
-            copy.start()
-        part = dot(sn[RP : RP + ROWS, i * CH : (i + 1) * CH], wq[i])
-        if i == 0:
-            qacc[...] = part
-        else:
-            qacc[...] += part
     for g in range(G):
         x = qacc[:, g * HD : (g + 1) * HD]
         x = x * cos_new + pltpu.roll(x, HD // 2, 1) * sin_new
@@ -295,14 +295,16 @@
         chunk = pos_row[:, j : j + HD].astype(F32)
         posb[j : j + HD, :] = jnp.transpose(jnp.broadcast_to(chunk, (HD, HD)))
 
+    TB = RP // 4
+
     def tables(i, carry):
-        at = pl.ds(pl.multiple_of(i * 16, 16), 16)
+        at = pl.ds(pl.multiple_of(i * TB, 8), TB)
         turned = posb[at, :] * freq
         ropec[at, :] = jnp.cos(turned)
         ropes[at, :] = jnp.sin(turned) * sign
         return carry
 
-    lax.fori_loop(0, RP // 16, tables, 0)
+    lax.fori_loop(0, RP // TB, tables, 0)
     my_len = jnp.sum(jnp.where(iota((1, n_p), 1) == me, plen, 0), axis=1, keepdims=True).astype(F32)
     for b in range(0, CTX, HD):
         first = b // 10 // 8 * 8

time: 37.6 us -> 36.8 us (0.979)
  Pallas kernels: 36.7 us -> 36 us
    pallas_call x1, Pallas kernels: 35.3 us -> 34.5 us  [per_device(): pl.pallas_call(functools.partial(kernel, dims), out_shape=(jax.ShapeDtype...]
where the time goes in v4:
time: 36.8 us; the launch traced here: 36.6 us
  Pallas kernels  36 us (98%)
  between operations  0.64 us (2%)
    pallas_call x1, Pallas kernels, per_device(): pl.pallas_call(functools.partial(kernel, dims), out_shape=(jax.ShapeDtype...  34.5 us
    pallas_call x1, Pallas kernels, per_device(): pl.pallas_call(finish, out_shape=(jax.ShapeDtypeStruct((CD, T, QW), BF16)...  1.49 us

profile of v4, /device:TPU:1, one launch (start us, length us, event | category | flops | bytes accessed | tf_op | source)
XLA Modules:
  0.0 36.6 jit_solution(16274021963850330676)
XLA Ops:
  0.6 34.5 %decode.1 = (bf16[32,896]{1,0:T(8,128)(2,1)}, f32[8,128]{1,0:T(8,128)}) custom-call(bf16[16,2,7168]{2,1,0:T(2,128)(2,1)} %nh_hbm.1, f32[1,7168]{1,0:T(1,128)} %bitcast.4, bf16[7168,896]{1,0:T(8,128)(2,1)} %wq_hbm.1, bf16[7168,128]{1,0:T(8,128)(2,1)} %wk_hbm.1, bf16[7168,128]{1,0:T(8,128)(2,1)} %wv_hbm.1, bf16[1,409,7168]{2,1,0:T(8,128)(2,1)} %hs_hbm.1, ...), custom_call_target="tpu_custom_call" | custom-call | tf_op jit(solution)/shard_map/decode/pallas_call | solution.py:610
  35.1 1.5 %finish.1 = (bf16[16,2,896]{2,1,0:T(2,128)(2,1)}, f32[16]{0:T(128)}) custom-call(bf16[32,896]{1,0:T(8,128)(2,1)} %get-tuple-element.4.rows_ref, f32[8,128]{1,0:T(8,128)} %get-tuple-element.5.line_ref), custom_call_target="tpu_custom_call" | custom-call | tf_op jit(solution)/shard_map/finish/pallas_call | solution.py:690
